TPU v7x, 32 devices: a whole 2x2x4 slice. The times are simulated.
32 devices in a mesh: batch: 4 (over x, core), seq: 8 (over z, y).
Axes of the slice: x: 2, y: 2, z: 4, core: 2. Of those that a mesh axis runs over, the one named last changes fastest.
Arguments:
- inputs: float32 [8, 2048, 512], P('batch', 'seq'), may hold values from -12 to 12
- norm_gain: float32 [512], replicated, may hold values from 0.25 to 1.75
- norm_bias: float32 [512], replicated, may hold values from -3 to 3
- query_weight: float32 [512, 512], replicated, may hold values from -0.25 to 0.25
- query_bias: float32 [512], replicated, may hold values from -3 to 3
- key_weight: float32 [512, 512], replicated, may hold values from -0.25 to 0.25
- value_weight: float32 [512, 512], replicated, may hold values from -0.25 to 0.25
- value_bias: float32 [512], replicated, may hold values from -3 to 3
- mixer_weight: float32 [512, 512], replicated, may hold values from -0.5 to 0.5
- mixer_bias: float32 [512], replicated, may hold values from -3 to 3
- final_gain: float32 [512], replicated, may hold values from 0.25 to 1.75
- final_bias: float32 [512], replicated, may hold values from -3 to 3
- inner_weight: float32 [512, 2048], replicated, may hold values from -0.25 to 0.25
- inner_bias: float32 [2048], replicated, may hold values from -3 to 3
- outer_weight: float32 [2048, 512], replicated, may hold values from -0.125 to 0.125
- outer_bias: float32 [512], replicated, may hold values from -3 to 3
- cotangent: float32 [8, 2048, 512], P('batch', 'seq'), may hold values from -6 to 6
Outputs:
- outputs: float32 [8, 2048, 512], P('batch', 'seq')
- inputs_grad: float32 [8, 2048, 512], P('batch', 'seq')
- norm_gain_grad: float32 [512], replicated
- norm_bias_grad: float32 [512], replicated
- query_weight_grad: float32 [512, 512], replicated
- query_bias_grad: float32 [512], replicated
- key_weight_grad: float32 [512, 512], replicated
- value_weight_grad: float32 [512, 512], replicated
- value_bias_grad: float32 [512], replicated
- mixer_weight_grad: float32 [512, 512], replicated
- mixer_bias_grad: float32 [512], replicated
- final_gain_grad: float32 [512], replicated
- final_bias_grad: float32 [512], replicated
- inner_weight_grad: float32 [512, 2048], replicated
- inner_bias_grad: float32 [2048], replicated
- outer_weight_grad: float32 [2048, 512], replicated
- outer_bias_grad: float32 [512], replicated
All inputs are finite; a program needn't handle non-finite values.
Results may differ from a plain program's by a relative error of at most 0.0003.
Values sent between devices are 32-bit elements; how exact they have to be, the bound alone decides.
No kernel may reach another device: no remote copies, remote signals or barrier semaphores. Data moves between devices by JAX's collectives and lax.ppermute only.
A program may use at most 192 MiB of HBM per device.

v0:
```python
import math
import jax
import jax.numpy as jnp
from jax import lax
from jax.sharding import PartitionSpec as P

HEADS = 8
highest = lax.Precision.HIGHEST
root_half = 0.7071067811865476
inv_root_two_pi = 0.3989422804014327


def extended_2(block, sides, width):
    for axis, dim in sides:
        count = lax.axis_size(axis)
        forward = [(i, i + 1) for i in range(count - 1)]
        backward = [(target, source) for source, target in forward]
        low = lax.ppermute(
            lax.slice_in_dim(block, block.shape[dim] - width, None, axis=dim), axis, forward
        )
        high = lax.ppermute(lax.slice_in_dim(block, 0, width, axis=dim), axis, backward)
        block = jnp.concatenate([low, block, high], axis=dim)
    return block


def from_partner(array, axis, apart):
    return lax.ppermute(array, axis, [(i, i ^ 1 << apart) for i in range(lax.axis_size(axis))])


def matmul(left_side, right_side):
    return jnp.dot(left_side, right_side, precision=highest)


def contract(formula, left_side, right_side):
    return jnp.einsum(formula, left_side, right_side, precision=highest)


def norm_forward(values, gain_vec, shift_vec):
    center = values - jnp.mean(values, axis=-1, keepdims=True)
    inverse = lax.rsqrt(jnp.mean(center * center, axis=-1, keepdims=True) + 1e-06)
    unit_rows = center * inverse
    return (unit_rows * gain_vec + shift_vec, unit_rows, inverse)


def norm_backward(grad_rows, unit_rows, inverse, gain_vec):
    grad_unit = grad_rows * gain_vec
    grad_input = inverse * (
        grad_unit
        - jnp.mean(grad_unit, axis=-1, keepdims=True)
        - unit_rows * jnp.mean(grad_unit * unit_rows, axis=-1, keepdims=True)
    )
    return (grad_input, jnp.sum(grad_rows * unit_rows, axis=0), jnp.sum(grad_rows, axis=0))


def pair_mean(values):
    lead_shape = values.shape
    return jnp.mean(values.reshape((lead_shape[0], lead_shape[1] // 2, 2) + lead_shape[2:]), axis=2)


def pair_spread(grad_rows):
    return jnp.repeat(grad_rows, 2, axis=1) * 0.5


def fold_runs(grad_rows, stride):
    lead_shape = grad_rows.shape
    return jnp.sum(
        grad_rows.reshape((lead_shape[0], lead_shape[1] // stride, stride) + lead_shape[2:]), axis=2
    )


def swap_halves(values):
    lead_shape = values.shape
    return values.reshape((lead_shape[0], lead_shape[1] // 2, 2) + lead_shape[2:])[
        :, :, ::-1
    ].reshape(lead_shape)


def split_heads(packed, heads):
    half_width = packed.shape[-1] // 2
    lead_shape = packed.shape[:-1] + (heads, half_width // heads)
    return (
        packed[..., :half_width].reshape(lead_shape),
        packed[..., half_width:].reshape(lead_shape),
    )


def join_heads(key_part, value_part):
    lead_shape = key_part.shape[:-2] + (-1,)
    return jnp.concatenate([key_part.reshape(lead_shape), value_part.reshape(lead_shape)], axis=-1)


def windows(extended, blocks):
    grouped = extended.reshape((extended.shape[0], blocks + 2, 16, extended.shape[-1]))
    return jnp.concatenate([grouped[:, :-2], grouped[:, 1:-1], grouped[:, 2:]], axis=2)


def unwindow(grad_window, blocks):
    summed = jnp.pad(grad_window[:, :, :16], ((0, 0), (0, 2), (0, 0), (0, 0)))
    summed = summed + jnp.pad(grad_window[:, :, 16:32], ((0, 0), (1, 1), (0, 0), (0, 0)))
    summed = summed + jnp.pad(grad_window[:, :, 32:], ((0, 0), (2, 0), (0, 0), (0, 0)))
    return summed.reshape((grad_window.shape[0], (blocks + 2) * 16, grad_window.shape[-1]))


def pairs_forward(queries, key_vecs, values, factor):
    weights = jnp.exp(contract("gbqhe,gbkhe->gbhqk", queries, key_vecs)) * factor
    numerator = contract("gbhqk,gbkhe->gbqhe", weights, values)
    denominator = jnp.transpose(jnp.sum(weights, axis=-1), (0, 1, 3, 2))
    return (numerator, denominator)


def pairs_backward(queries, key_vecs, values, factor, grad_numerator, grad_denominator):
    weights = jnp.exp(contract("gbqhe,gbkhe->gbhqk", queries, key_vecs)) * factor
    grad_scores = weights * (
        contract("gbqhe,gbkhe->gbhqk", grad_numerator, values)
        + jnp.transpose(grad_denominator, (0, 1, 3, 2))[..., None]
    )
    grad_values = contract("gbhqk,gbqhe->gbkhe", weights, grad_numerator)
    grad_queries = contract("gbhqk,gbkhe->gbqhe", grad_scores, key_vecs)
    grad_keys = contract("gbhqk,gbqhe->gbkhe", grad_scores, queries)
    return (grad_queries, grad_keys, grad_values)


def per_device(
    inputs,
    norm_gain,
    norm_bias,
    query_weight,
    query_bias,
    key_weight,
    value_weight,
    value_bias,
    mixer_weight,
    mixer_bias,
    final_gain,
    final_bias,
    inner_weight,
    inner_bias,
    outer_weight,
    outer_bias,
    cotangent,
):
    groups, span_tokens, model_width = inputs.shape
    heads = HEADS
    head_size = model_width // heads
    row_total = groups * span_tokens
    head_scale = 1.0 / math.sqrt(head_size)
    flat_inputs = inputs.reshape(row_total, model_width)
    normed, unit_first, inverse_first = norm_forward(flat_inputs, norm_gain, norm_bias)
    queries = (matmul(normed, query_weight) + query_bias) * head_scale
    key_vecs = matmul(normed, key_weight)
    values = matmul(normed, value_weight) + value_bias
    scaled = queries.reshape(groups, span_tokens, heads, head_size)
    packed = jnp.concatenate([key_vecs, values], axis=-1).reshape(
        groups, span_tokens, 2 * model_width
    )
    seq_index = lax.axis_index("seq")
    seq_count = lax.axis_size("seq")
    crossing = seq_count.bit_length() - 1
    local_top = 0
    while 32 * 2 ** (local_top + 1) <= span_tokens:
        local_top = local_top + 1
    top_level = local_top + crossing
    query_levels = [scaled]
    for level_index in range(top_level):
        query_levels.append(pair_mean(query_levels[-1]))
    kv_levels = [packed]
    for level_index in range(local_top + 1):
        kv_levels.append(pair_mean(kv_levels[-1]))
    blocks = span_tokens // 16
    extended = extended_2(packed, (("seq", 1),), 16)
    win_keys, win_values = split_heads(windows(extended, blocks), heads)
    slot_ids = jnp.arange(48)
    block_ids = jnp.arange(blocks)
    is_valid = ((block_ids[:, None] > 0) | (slot_ids[None, :] >= 16) | (seq_index > 0)) & (
        (block_ids[:, None] < blocks - 1) | (slot_ids[None, :] < 32) | (seq_index < seq_count - 1)
    )
    validity = is_valid.astype(jnp.float32)[None, :, None, None, :]
    block_queries = scaled.reshape(groups, blocks, 16, heads, head_size)
    numerator, denominator = pairs_forward(block_queries, win_keys, win_values, validity)
    numerator = numerator.reshape(groups, span_tokens, heads, head_size)
    denominator = denominator.reshape(groups, span_tokens, heads)
    partners = []
    own_block = kv_levels[local_top + 1]
    for level_bit in range(crossing):
        partner = from_partner(own_block, "seq", level_bit)
        partners.append(partner)
        if level_bit + 1 < crossing:
            is_lower = seq_index // 2**level_bit % 2 == 0
            joined = jnp.where(
                is_lower,
                jnp.concatenate([own_block, partner], axis=1),
                jnp.concatenate([partner, own_block], axis=1),
            )
            own_block = pair_mean(joined)

    def level_operands(level_index):
        stride = 2**level_index
        if level_index <= local_top:
            block_count = span_tokens // stride // 16
            level_queries = query_levels[level_index].reshape(
                groups, block_count, 16, heads, head_size
            )
            partner_kv = swap_halves(
                kv_levels[level_index].reshape(groups, block_count, 16, 2 * model_width)
            )
        else:
            level_queries = query_levels[level_index].reshape(
                groups, 1, span_tokens // stride, heads, head_size
            )
            partner_kv = partners[level_index - local_top - 1].reshape(
                groups, 1, 16, 2 * model_width
            )
        key_part, value_part = split_heads(partner_kv, heads)
        return (level_queries, key_part, value_part, float(stride))

    for level_index in range(1, top_level + 1):
        stride = 2**level_index
        level_queries, key_part, value_part, factor = level_operands(level_index)
        part_num, part_den = pairs_forward(level_queries, key_part, value_part, factor)
        numerator = numerator + jnp.repeat(
            part_num.reshape(groups, span_tokens // stride, heads, head_size), stride, axis=1
        )
        denominator = denominator + jnp.repeat(
            part_den.reshape(groups, span_tokens // stride, heads), stride, axis=1
        )
    mixed = numerator / denominator[..., None]
    mixed_flat = mixed.reshape(row_total, model_width)
    middle = flat_inputs + matmul(mixed_flat, mixer_weight) + mixer_bias
    final_normed, unit_second, inverse_second = norm_forward(middle, final_gain, final_bias)
    inner_act = matmul(final_normed, inner_weight) + inner_bias
    cumulative = 0.5 * (1.0 + lax.erf(inner_act * root_half))
    hidden = inner_act * cumulative
    outputs = middle + matmul(hidden, outer_weight) + outer_bias
    grad_out = cotangent.reshape(row_total, model_width)
    outer_weight_grad = matmul(hidden.T, grad_out)
    outer_bias_grad = jnp.sum(grad_out, axis=0)
    grad_inner = matmul(grad_out, outer_weight.T) * (
        cumulative + inner_act * jnp.exp(-0.5 * inner_act * inner_act) * inv_root_two_pi
    )
    inner_weight_grad = matmul(final_normed.T, grad_inner)
    inner_bias_grad = jnp.sum(grad_inner, axis=0)
    grad_middle_part, final_gain_grad, final_bias_grad = norm_backward(
        matmul(grad_inner, inner_weight.T), unit_second, inverse_second, final_gain
    )
    grad_middle = grad_out + grad_middle_part
    mixer_weight_grad = matmul(mixed_flat.T, grad_middle)
    mixer_bias_grad = jnp.sum(grad_middle, axis=0)
    grad_attend = matmul(grad_middle, mixer_weight.T).reshape(groups, span_tokens, heads, head_size)
    grad_numerator = grad_attend / denominator[..., None]
    grad_denominator = -jnp.sum(grad_attend * mixed, axis=-1) / denominator
    zero_queries, grad_win_keys, grad_win_values = pairs_backward(
        block_queries,
        win_keys,
        win_values,
        validity,
        grad_numerator.reshape(groups, blocks, 16, heads, head_size),
        grad_denominator.reshape(groups, blocks, 16, heads),
    )
    grad_query_levels = [zero_queries.reshape(groups, span_tokens, heads, head_size)]
    grad_extended = unwindow(join_heads(grad_win_keys, grad_win_values), blocks)
    rims = jnp.concatenate([grad_extended[:, :16], grad_extended[:, span_tokens + 16 :]], axis=1)
    returned = extended_2(rims, (("seq", 1),), 16)
    grad_packed_zero = grad_extended[:, 16 : span_tokens + 16]
    grad_packed_zero = grad_packed_zero.at[:, :16].add(returned[:, :16])
    grad_packed_zero = grad_packed_zero.at[:, span_tokens - 16 :].add(returned[:, 48:])
    grad_kv_levels = [grad_packed_zero]
    grad_partners = []
    for level_index in range(1, top_level + 1):
        stride = 2**level_index
        level_queries, key_part, value_part, factor = level_operands(level_index)
        level_grad_num = fold_runs(grad_numerator, stride).reshape(level_queries.shape)
        level_grad_den = fold_runs(grad_denominator, stride).reshape(level_queries.shape[:-1])
        grad_level_q, grad_level_k, grad_level_v = pairs_backward(
            level_queries, key_part, value_part, factor, level_grad_num, level_grad_den
        )
        grad_query_levels.append(
            grad_level_q.reshape(groups, span_tokens // stride, heads, head_size)
        )
        joined_grad = join_heads(grad_level_k, grad_level_v)
        if level_index <= local_top:
            grad_kv_levels.append(
                swap_halves(joined_grad).reshape(groups, span_tokens // stride, 2 * model_width)
            )
        else:
            grad_partners.append(joined_grad.reshape(groups, 16, 2 * model_width))
    grad_next = None
    for level_bit in range(crossing - 1, -1, -1):
        grad_partner = grad_partners[level_bit]
        if level_bit + 1 < crossing:
            spread = pair_spread(grad_next)
            is_lower = seq_index // 2**level_bit % 2 == 0
            grad_mine = jnp.where(is_lower, spread[:, :16], spread[:, 16:])
            grad_partner = grad_partner + jnp.where(is_lower, spread[:, 16:], spread[:, :16])
        else:
            grad_mine = jnp.zeros_like(grad_partner)
        grad_next = grad_mine + from_partner(grad_partner, "seq", level_bit)
    grad_kv = grad_next
    for level_index in range(local_top, -1, -1):
        grad_kv = pair_spread(grad_kv) + grad_kv_levels[level_index]
    grad_query = grad_query_levels[top_level]
    for level_index in range(top_level - 1, -1, -1):
        grad_query = pair_spread(grad_query) + grad_query_levels[level_index]
    grad_queries = grad_query.reshape(row_total, model_width) * head_scale
    grad_keys = grad_kv[..., :model_width].reshape(row_total, model_width)
    grad_values = grad_kv[..., model_width:].reshape(row_total, model_width)
    query_weight_grad = matmul(normed.T, grad_queries)
    query_bias_grad = jnp.sum(grad_queries, axis=0)
    key_weight_grad = matmul(normed.T, grad_keys)
    value_weight_grad = matmul(normed.T, grad_values)
    value_bias_grad = jnp.sum(grad_values, axis=0)
    grad_normed = (
        matmul(grad_queries, query_weight.T)
        + matmul(grad_keys, key_weight.T)
        + matmul(grad_values, value_weight.T)
    )
    grad_first, norm_gain_grad, norm_bias_grad = norm_backward(
        grad_normed, unit_first, inverse_first, norm_gain
    )
    inputs_grad = grad_middle + grad_first
    (
        norm_gain_grad,
        norm_bias_grad,
        query_weight_grad,
        query_bias_grad,
        key_weight_grad,
        value_weight_grad,
        value_bias_grad,
        mixer_weight_grad,
        mixer_bias_grad,
        final_gain_grad,
        final_bias_grad,
        inner_weight_grad,
        inner_bias_grad,
        outer_weight_grad,
        outer_bias_grad,
    ) = lax.psum(
        (
            norm_gain_grad,
            norm_bias_grad,
            query_weight_grad,
            query_bias_grad,
            key_weight_grad,
            value_weight_grad,
            value_bias_grad,
            mixer_weight_grad,
            mixer_bias_grad,
            final_gain_grad,
            final_bias_grad,
            inner_weight_grad,
            inner_bias_grad,
            outer_weight_grad,
            outer_bias_grad,
        ),
        ("batch", "seq"),
    )
    return (
        outputs.reshape(groups, span_tokens, model_width),
        inputs_grad.reshape(groups, span_tokens, model_width),
        norm_gain_grad,
        norm_bias_grad,
        query_weight_grad,
        query_bias_grad,
        key_weight_grad,
        value_weight_grad,
        value_bias_grad,
        mixer_weight_grad,
        mixer_bias_grad,
        final_gain_grad,
        final_bias_grad,
        inner_weight_grad,
        inner_bias_grad,
        outer_weight_grad,
        outer_bias_grad,
    )


def solution(mesh):
    return jax.shard_map(
        per_device,
        mesh=mesh,
        in_specs=(
            P("batch", "seq", None),
            P(),
            P(),
            P(),
            P(),
            P(),
            P(),
            P(),
            P(),
            P(),
            P(),
            P(),
            P(),
            P(),
            P(),
            P(),
            P("batch", "seq", None),
        ),
        out_specs=(
            P("batch", "seq", None),
            P("batch", "seq", None),
            P(),
            P(),
            P(),
            P(),
            P(),
            P(),
            P(),
            P(),
            P(),
            P(),
            P(),
            P(),
            P(),
            P(),
            P(),
        ),
        check_vma=False,
    )
```

profile of v0, /device:TPU:0, one launch (start us, length us, event | category | flops | bytes accessed | tf_op | source)
XLA Modules:
  0.0 826.7 jit_solution(6064375507251882588)
XLA Ops:
  22.9 5.1 reduce_sum.457
  56.2 4.1 fusion.33
  98.7 4.3 fusion.162
  151.9 5.6 reshape.1074
  157.5 15.4 %fusion.161 = (f32[2,16,8,16]{3,2,1,0:T(8,128)S(1)}, f32[2,16,8,16,48]{4,3,2,1,0:T(8,128)}) fusion(f32[16,48]{1,0:T(8,128)S(1)} %and_convert_fusion, f32[2,16,48,8,64]{4,3,2,1,0:T(8,128)} %reshape.1074, f32[2,16,16,8,64]{4,3,2,1,0:T(8,128)} %reshape_reshape.24), kind=kOutput, calls=%fused_computation.291 | convolution fusion | flops 151384064 | bytes 5000192 | tf_op jit(solution)/shard_map/gbqhe,gbkhe->gbhqk/dot_general | solution.py:35
  181.1 4.5 collective-permute-start.3
  185.7 5.6 reshape.1073
  191.3 9.1 %fusion.23 = f32[2,16,16,8,64]{4,2,3,1,0:T(8,128)S(1)} fusion(f32[2,16,8,16,48]{4,3,2,1,0:T(8,128)} %get-tuple-element.122, f32[2,16,48,8,64]{4,3,2,1,0:T(8,128)} %reshape.1073), kind=kOutput, calls=%fused_computation.35 | convolution fusion | flops 150994944 | bytes 4980736 | tf_op jit(solution)/shard_map/gbhqk,gbkhe->gbqhe/dot_general | solution.py:35
  242.8 4.2 add_divide_fusion
  249.6 6.9 fusion.65
  256.6 9.1 %fusion.164 = (f32[2048]{0:T(1024)}, f32[512,2048]{1,0:T(8,128)S(1)}) fusion(f32[512,2048]{1,0:T(8,128)S(1)} %fusion.65, f32[2048]{0:T(1024)S(1)} %copy-done.166, f32[512,512]{1,0:T(8,128)S(1)} %bitcast.532, f32[2048,512]{1,0:T(8,128)S(1)} %copy-done.165), kind=kOutput, calls=%fused_computation.294 | convolution fusion | flops 6453983232 | bytes 13647872 | tf_op jit(solution)/shard_map/dot_general | solution.py:31
  265.7 8.8 %fusion.64 = f32[512,2048]{1,0:T(8,128)} fusion(f32[512,2048]{1,0:T(8,128)S(1)} %get-tuple-element.131, f32[512,512]{1,0:T(8,128)S(1)} %get-tuple-element.126, f32[512]{0:T(512)S(1)} %copy-done.141, f32[512]{0:T(512)S(1)} %copy-done.133, f32[512]{0:T(512)S(1)} %add_rsqrt_fusion, f32[512]{0:T(512)S(1)} %broadcast_multiply_fusion.15), kind=kOutput, calls=%fused_computation.134 | convolution fusion | flops 6443499520 | bytes 9445376 | tf_op jit(solution)/shard_map/dot_general | solution.py:31
  274.5 7.7 multiply_reduce_fusion
  298.2 3.6 reshape.1135
  301.8 4.3 multiply_reduce_fusion.3
  308.9 12.6 %convolution_bitcast_fusion = f32[2,16,48,8,64]{4,2,3,1,0:T(8,128)S(1)} fusion(f32[2,16,8,16,48]{4,3,2,1,0:T(8,128)} %get-tuple-element.122, f32[2,16,16,8,64]{4,3,2,1,0:T(8,128)} %reshape.1145, f32[2,16,16,8]{2,3,1,0:T(8,128)S(1)} %get-tuple-element.69), kind=kOutput, calls=%fused_computation.17 | convolution fusion | flops 151257088 | bytes 4997120 | tf_op jit(solution)/shard_map/gbhqk,gbqhe->gbkhe/dot_general | solution.py:35
  321.5 5.2 copy.830
  326.7 6.2 reshape.1182
  332.9 14.5 %add_multiply_fusion.2 = f32[2,16,8,16,48]{4,3,2,1,0:T(8,128)S(1)} fusion(f32[2,16,8,16,48]{4,3,2,1,0:T(8,128)} %get-tuple-element.122, f32[2,16,48,8,64]{4,3,2,1,0:T(8,128)} %reshape.1073, f32[2,16,8,16]{3,2,1,0:T(8,128)} %get-tuple-element.68, f32[2,16,16,8,64]{4,3,2,1,0:T(8,128)} %reshape.1145, f32[2,16,16,8]{2,3,1,0:T(8,128)S(1)} %get-tuple-element.69), kind=kOutput, calls=%fused_computation.25 | convolution fusion | flops 151650304 | bytes 5799936 | tf_op jit(solution)/shard_map/gbqhe,gbkhe->gbhqk/dot_general | solution.py:35
  348.8 10.1 %convolution_bitcast_fusion.1 = f32[2,16,48,8,64]{4,2,3,1,0:T(8,128)S(1)} fusion(f32[2,16,8,16,48]{4,3,2,1,0:T(8,128)S(1)} %add_multiply_fusion.2, f32[2,16,16,8,64]{4,3,2,1,0:T(8,128)S(1)} %copy-done.10), kind=kOutput, calls=%fused_computation.18 | convolution fusion | flops 150994944 | bytes 4980736 | tf_op jit(solution)/shard_map/gbhqk,gbqhe->gbkhe/dot_general | solution.py:35
  358.9 5.5 copy.829
  364.4 6.3 reshape.1181
  405.4 4.0 fusion.30
  443.1 10.5 %fusion.28 = f32[2048,512]{1,0:T(8,128)} fusion(f32[512,512]{1,0:T(8,128)S(1)} %bitcast.533, f32[512,2048]{1,0:T(8,128)} %copy-done.27, f32[2048]{0:T(1024)S(1)} %copy-done.167), kind=kOutput, calls=%fused_computation.36 | convolution fusion | flops 6447693824 | bytes 9445376 | tf_op jit(solution)/shard_map/dot_general | solution.py:31
  492.5 7.4 fusion.142
  508.9 4.0 fusion.166
  559.6 3.7 mul.399
  574.9 3.8 copy.806
  581.6 3.6 fusion.53
  585.3 10.9 %fusion.35 = f32[512,512]{1,0:T(8,128)} fusion(f32[512,512]{1,0:T(8,128)S(1)} %get-tuple-element.126, f32[2048,512]{1,0:T(8,128)} %param.35, f32[512,2048]{1,0:T(8,128)S(1)} %copy-done.28, f32[2048]{0:T(1024)S(1)} %copy-done.168, f32[512]{0:T(512)S(1)} %copy-done.169), kind=kOutput, calls=%fused_computation.56 | convolution fusion | flops 6448218112 | bytes 10496000 | tf_op jit(solution)/shard_map/dot_general | solution.py:31
  602.8 41.3 %all-reduce.3 = (f32[512]{0:T(512)}, f32[512]{0:T(512)}, f32[512]{0:T(512)}, f32[512]{0:T(512)}, f32[512]{0:T(512)}, /*index=5*/f32[512]{0:T(512)}, f32[512]{0:T(512)}, f32[2048]{0:T(1024)}, f32[512]{0:T(512)}) all-reduce(f32[512]{0:T(512)S(1)} %get-tuple-element.43, ...), channel_id=1, replica_groups=mesh['batch'=4,'seq'=8] {'batch','seq'}, use_global_device_ids=true, to_apply=%region_41.42 | all-reduce | flops 6144 | bytes 49152 | tf_op jit(solution)/shard_map/psum | solution.py:336
  646.7 161.7 %all-reduce.7.cloned.1.call-done = (f32[512,512]{1,0:T(8,128)}, f32[512,512]{1,0:T(8,128)}, f32[512,512]{1,0:T(8,128)}, f32[512,512]{1,0:T(8,128)}, f32[512,2048]{1,0:T(8,128)}, /*index=5*/f32[2048,512]{1,0:T(8,128)}) async-done(((f32[512,512]{1,0:T(8,128)}, f32[512,512]{1,0:T(8,128)}, f32[512,512]{1,0:T(8,128)}, f32[512,512]{1,0:T(8,128)}, f32[512,2048]{1,0:T(8,128)}, /*index=5*/f32[2048,512]{1,0:T(8,128)}), ...) | async-done | bytes 12582928 | tf_op jit(solution)/shard_map/psum | solution.py:336
  (707 shorter events, 400.3 us)
Async XLA Ops:
  7.2 801.2 %all-reduce.7.cloned.1.call-start = ((), (), s32[]{:S(2)}) async-start(), calls=%async_computation | async-start | bytes 25165824 | tf_op jit(solution)/shard_map/psum | solution.py:336
  10.7 45.5 %copy-start.3 = (f32[512,512]{1,0:T(8,128)}, f32[512,512]{1,0:T(8,128)S(1)}, u32[]{:S(2)}) copy-start(f32[512,512]{1,0:T(8,128)S(1)} %fusion.52) | copy-start | bytes 3145732
  42.1 18.2 %copy-start.59 = (f32[2,32,1024]{2,1,0:T(8,128)}, f32[2,32,1024]{2,1,0:T(8,128)S(1)}, u32[]{:S(2)}) copy-start(f32[2,32,1024]{2,1,0:T(8,128)S(1)} %reduce_sum.463) | copy-start | bytes 786436
  46.6 128.9 %collective-permute-start.2 = (f32[2,16,1024]{2,1,0:T(8,128)}, f32[2,16,1024]{2,1,0:T(8,128)}, u32[]{:S(2)}, u32[]{:S(2)}) collective-permute-start(f32[2,16,1024]{2,1,0:T(8,128)} %broadcast_multiply_fusion.9), channel_id=1, source_target_pairs={{0,1},{1,0},{2,3},{3,2},{4,5},{5,4},{6,7},{7,6},{8,9},{9,8},{10,11... | collective-permute-start | bytes 393224 | tf_op jit(solution)/shard_map/ppermute | solution.py:27
  51.3 93.4 %collective-permute-start = (f32[2,16,1024]{2,1,0:T(8,128)}, f32[2,16,1024]{2,1,0:T(8,128)}, u32[]{:S(2)}, u32[]{:S(2)}) collective-permute-start(f32[2,16,1024]{2,1,0:T(8,128)} %get-tuple-element.93), channel_id=1, source_target_pairs={{0,1},{1,2},{2,3},{3,4},{4,5},{5,6},{6,7},{8,9},{9,10},{10,11},{11... | collective-permute-start | bytes 393224 | tf_op jit(solution)/shard_map/ppermute | solution.py:18
  53.8 90.9 %collective-permute-start.1 = (f32[2,16,1024]{2,1,0:T(8,128)}, f32[2,16,1024]{2,1,0:T(8,128)}, u32[]{:S(2)}, u32[]{:S(2)}) collective-permute-start(f32[2,16,1024]{2,1,0:T(8,128)} %get-tuple-element.94), channel_id=1, source_target_pairs={{1,0},{2,1},{3,2},{4,3},{5,4},{6,5},{7,6},{9,8},{10,9},{11,10},{12... | collective-permute-start | bytes 393224 | tf_op jit(solution)/shard_map/ppermute | solution.py:21
  69.3 29.4 %copy-start.17 = (f32[2,128,8,64]{3,2,1,0:T(8,128)}, f32[2,128,8,64]{3,2,1,0:T(8,128)S(1)}, u32[]{:S(2)}) copy-start(f32[2,128,8,64]{3,2,1,0:T(8,128)S(1)} %broadcast_multiply_fusion.1) | copy-start | bytes 1572868
  84.8 91.6 %copy-start.66 = (f32[2,16,8,64]{3,2,1,0:T(8,128)}, f32[2,16,8,64]{3,2,1,0:T(8,128)S(1)}, u32[]{:S(2)}) copy-start(f32[2,16,8,64]{3,2,1,0:T(8,128)S(1)} %reduce_sum.467) | copy-start | bytes 196612
  176.8 28.7 %copy-start.68 = (f32[2,8,16,16]{2,3,1,0:T(8,128)}, f32[2,8,16,16]{2,3,1,0:T(8,128)S(1)}, u32[]{:S(2)}) copy-start(f32[2,8,16,16]{2,3,1,0:T(8,128)S(1)} %get-tuple-element.116) | copy-start | bytes 49156
  181.1 36.7 %collective-permute-start.3 = (f32[2,16,1024]{2,1,0:T(8,128)S(1)}, f32[2,16,1024]{2,1,0:T(8,128)S(1)}, u32[]{:S(2)}, u32[]{:S(2)}) collective-permute-start(f32[2,16,1024]{2,1,0:T(8,128)S(1)} %broadcast_multiply_fusion.8), channel_id=1, source_target_pairs={{0,2},{1,3},{2,0},{3,1},{4,6},{5,7},{6,4},{7,5},{8,10},{9,11},{10,... | collective-permute-start | bytes 393224 | tf_op jit(solution)/shard_map/ppermute | solution.py:27
  218.4 11.8 %copy-start.136 = (f32[2,8,8]{2,1,0:T(8,128)}, f32[2,8,8]{2,1,0:T(8,128)S(1)}, u32[]{:S(2)}) copy-start(f32[2,8,8]{2,1,0:T(8,128)S(1)} %get-tuple-element.113) | copy-start | bytes 1540
  219.8 11.8 %collective-permute-start.4 = (f32[2,16,1024]{2,1,0:T(8,128)S(1)}, f32[2,16,1024]{2,1,0:T(8,128)S(1)}, u32[]{:S(2)}, u32[]{:S(2)}) collective-permute-start(f32[2,16,1024]{2,1,0:T(8,128)S(1)} %broadcast_multiply_fusion.7), channel_id=1, source_target_pairs={{0,4},{1,5},{2,6},{3,7},{4,0},{5,1},{6,2},{7,3},{8,12},{9,13},{10,... | collective-permute-start | bytes 393224 | tf_op jit(solution)/shard_map/ppermute | solution.py:27
  232.2 74.7 %copy-start.129 = (f32[2,8,4]{1,2,0:T(4,128)}, f32[2,8,4]{1,2,0:T(4,128)S(1)}, u32[]{:S(2)}) copy-start(f32[2,8,4]{1,2,0:T(4,128)S(1)} %copy.712) | copy-start | bytes 772
  332.9 15.9 %copy-start.10 = (f32[2,16,16,8,64]{4,3,2,1,0:T(8,128)S(1)}, f32[2,16,16,8,64]{4,3,2,1,0:T(8,128)}, u32[]{:S(2)}) copy-start(f32[2,16,16,8,64]{4,3,2,1,0:T(8,128)} %reshape_reshape.24) | copy-start | bytes 3145732
  432.2 11.0 %copy-start.167 = (f32[2048]{0:T(1024)S(1)}, f32[2048]{0:T(1024)}, u32[]{:S(2)}) copy-start(f32[2048]{0:T(1024)} %param.34) | copy-start | bytes 24580
  443.1 14.7 %copy-start.47 = (f32[2,8,16,8,64]{4,2,3,1,0:T(8,128)S(1)}, f32[2,8,16,8,64]{4,2,3,1,0:T(8,128)}, u32[]{:S(2)}) copy-start(f32[2,8,16,8,64]{4,2,3,1,0:T(8,128)} %convolution_bitcast_fusion.4) | copy-start | bytes 1572868
  453.6 78.8 %collective-permute-start.8 = (f32[2,16,1024]{2,1,0:T(8,128)}, f32[2,16,1024]{2,1,0:T(8,128)}, u32[]{:S(2)}, u32[]{:S(2)}) collective-permute-start(f32[2,16,1024]{2,1,0:T(8,128)} %get-tuple-element.86), channel_id=1, source_target_pairs={{0,1},{1,2},{2,3},{3,4},{4,5},{5,6},{6,7},{8,9},{9,10},{10,11},{11... | collective-permute-start | bytes 393224 | tf_op jit(solution)/shard_map/ppermute | solution.py:18
  456.5 82.8 %collective-permute-start.9 = (f32[2,16,1024]{2,1,0:T(8,128)}, f32[2,16,1024]{2,1,0:T(8,128)}, u32[]{:S(2)}, u32[]{:S(2)}) collective-permute-start(f32[2,16,1024]{2,1,0:T(8,128)} %get-tuple-element.85), channel_id=1, source_target_pairs={{1,0},{2,1},{3,2},{4,3},{5,4},{6,5},{7,6},{9,8},{10,9},{11,10},{12... | collective-permute-start | bytes 393224 | tf_op jit(solution)/shard_map/ppermute | solution.py:21
  471.1 14.4 %copy-start.69 = (f32[2,8,16,16]{2,3,1,0:T(8,128)S(1)}, f32[2,8,16,16]{2,3,1,0:T(8,128)}, u32[]{:S(2)}) copy-start(f32[2,8,16,16]{2,3,1,0:T(8,128)} %copy-done.68) | copy-start | bytes 49156
  471.1 14.3 %copy-start.75 = (f32[2,16,8,64]{3,2,1,0:T(8,128)S(1)}, f32[2,16,8,64]{3,2,1,0:T(8,128)}, u32[]{:S(2)}) copy-start(f32[2,16,8,64]{3,2,1,0:T(8,128)} %fusion.140) | copy-start | bytes 196612
  471.2 15.9 %copy-start.79 = (f32[2,16,8,64]{3,2,1,0:T(8,128)S(1)}, f32[2,16,8,64]{3,2,1,0:T(8,128)}, u32[]{:S(2)}) copy-start(f32[2,16,8,64]{3,2,1,0:T(8,128)} %copy-done.78) | copy-start | bytes 196612
  471.9 56.5 %collective-permute-start.5 = (f32[2,16,1024]{2,1,0:T(8,128)}, f32[2,16,1024]{2,1,0:T(8,128)}, u32[]{:S(2)}, u32[]{:S(2)}) collective-permute-start(f32[2,16,1024]{2,1,0:T(8,128)} %maximum_bitcast_fusion), channel_id=1, source_target_pairs={{0,4},{1,5},{2,6},{3,7},{4,0},{5,1},{6,2},{7,3},{8,12},{9,13},{10,... | collective-permute-start | bytes 393224 | tf_op jit(solution)/shard_map/ppermute | solution.py:27
  476.4 11.2 %copy-start.46 = (f32[2,8,16,8,64]{4,2,3,1,0:T(8,128)S(1)}, f32[2,8,16,8,64]{4,2,3,1,0:T(8,128)}, u32[]{:S(2)}) copy-start(f32[2,8,16,8,64]{4,2,3,1,0:T(8,128)} %convolution_bitcast_fusion.6) | copy-start | bytes 1572868
  514.0 12.4 %copy-start.107 = (f32[2,1,16,8,64]{4,2,3,0,1:T(8,128)S(1)}, f32[2,1,16,8,64]{4,2,3,0,1:T(8,128)}, u32[]{:S(2)}) copy-start(f32[2,1,16,8,64]{4,2,3,0,1:T(8,128)} %convolution_bitcast_fusion.16) | copy-start | bytes 196612
  514.0 14.1 %copy-start.67 = (f32[2,16,8,64]{3,2,1,0:T(8,128)S(1)}, f32[2,16,8,64]{3,2,1,0:T(8,128)}, u32[]{:S(2)}) copy-start(f32[2,16,8,64]{3,2,1,0:T(8,128)} %copy-done.66) | copy-start | bytes 196612
  514.0 14.1 %copy-start.86 = (f32[2,8,16,16]{2,3,1,0:T(8,128)S(1)}, f32[2,8,16,16]{2,3,1,0:T(8,128)}, u32[]{:S(2)}) copy-start(f32[2,8,16,16]{2,3,1,0:T(8,128)} %copy-done.85) | copy-start | bytes 49156
  532.2 5.0 collective-permute-start.6
  539.2 5.0 collective-permute-start.7
  599.4 44.7 %copy-start.2 = (f32[2,256,512]{2,1,0:T(8,128)S(1)}, f32[2,256,512]{2,1,0:T(8,128)}, u32[]{:S(2)}) copy-start(f32[2,256,512]{2,1,0:T(8,128)} %param.21) | copy-start | bytes 3145732
  599.4 44.7 %copy-start.16 = (f32[512,512]{1,0:T(8,128)S(1)}, f32[512,512]{1,0:T(8,128)}, u32[]{:S(2)}) copy-start(f32[512,512]{1,0:T(8,128)} %copy-done.14) | copy-start | bytes 3145732
  599.4 44.7 %copy-start.152 = (f32[1,2,2,128]{3,1,2,0:T(2,128)S(1)}, f32[1,2,2,128]{3,1,2,0:T(2,128)}, u32[]{:S(2)}) copy-start(f32[1,2,2,128]{3,1,2,0:T(2,128)} %copy-done.151) | copy-start | bytes 6148
  599.4 44.7 %copy-start.154 = (f32[1,2,2,128]{3,1,2,0:T(2,128)S(1)}, f32[1,2,2,128]{3,1,2,0:T(2,128)}, u32[]{:S(2)}) copy-start(f32[1,2,2,128]{3,1,2,0:T(2,128)} %copy-done.153) | copy-start | bytes 6148
  (151 other events, 619.4 us)
Sparse Core Ops, SparseCore 0:
  571.8 236.6 all-reduce.6
where the time goes:
time: 835 us; the launch traced here: 827 us
  local copies, waits for them, and re-layouts  275 us (33%)
  matrix products  208 us (25%)
  waiting for transfers between devices  168 us (20%)
  other arithmetic  95.3 us (11%)
  blocking collectives  41.3 us (5%)
  starting transfers between devices  21.5 us (3%)
  between operations  16.8 us (2%)
    psum x1, waiting for transfers between devices, per_device(): lax.psum((norm_gain_grad, norm_bias_grad, query_weight_grad, query_bias_g...  162 us
    dot_general x42, matrix products, contract(): return jnp.einsum(formula, left_side, right_side, precision=highest)  121 us
    dot_general x18, matrix products, matmul(): return jnp.dot(left_side, right_side, precision=highest)  87.1 us
    psum x1, blocking collectives, per_device(): lax.psum((norm_gain_grad, norm_bias_grad, query_weight_grad, query_bias_g...  41.3 us
    reshape x12, local copies, waits for them, and re-layouts, per_device(): jnp.repeat(part_num.reshape(groups, span_tokens // stride, heads, head_si...  36.1 us
    transpose x22, local copies, waits for them, and re-layouts, contract(): return jnp.einsum(formula, left_side, right_side, precision=highest)  27 us
    unnamed x356, local copies, waits for them, and re-layouts  26 us
    reduce_sum x12, other arithmetic, pair_mean(): jnp.mean(values.reshape((lead_shape[0], lead_shape[1] // 2, 2) + lead_sha...  19.6 us
  transfers between devices with their start and end apart: 11, of which 3 were waited for; matrix products, arithmetic and copies ran while one was open for 32% of the time, Pallas kernels for 0%

commit v1 on v0

--- a/solution.py
+++ b/solution.py
@@ -334,24 +334,27 @@
         outer_weight_grad,
         outer_bias_grad,
     ) = lax.psum(
-        (
-            norm_gain_grad,
-            norm_bias_grad,
-            query_weight_grad,
-            query_bias_grad,
-            key_weight_grad,
-            value_weight_grad,
-            value_bias_grad,
-            mixer_weight_grad,
-            mixer_bias_grad,
-            final_gain_grad,
-            final_bias_grad,
-            inner_weight_grad,
-            inner_bias_grad,
-            outer_weight_grad,
-            outer_bias_grad,
+        lax.psum(
+            (
+                norm_gain_grad,
+                norm_bias_grad,
+                query_weight_grad,
+                query_bias_grad,
+                key_weight_grad,
+                value_weight_grad,
+                value_bias_grad,
+                mixer_weight_grad,
+                mixer_bias_grad,
+                final_gain_grad,
+                final_bias_grad,
+                inner_weight_grad,
+                inner_bias_grad,
+                outer_weight_grad,
+                outer_bias_grad,
+            ),
+            "seq",
         ),
-        ("batch", "seq"),
+        "batch",
     )
     return (
         outputs.reshape(groups, span_tokens, model_width),

time: 835 us -> 1230 us (1.47)
  waiting for transfers between devices: 168 us -> 553 us
    psum x1, waiting for transfers between devices: 162 us -> 402 us  [per_device(): lax.psum((norm_gain_grad, norm_bias_grad, query_weight_grad, query_bias_g...]
    psum x0 -> x1, waiting for transfers between devices: none -> 144 us  [per_device(): lax.psum(lax.psum((norm_gain_grad, norm_bias_grad, query_weight_grad, que...]
  transfers between devices with their start and end apart: 11 -> 12, of which waited for: 3 -> 4; matrix products, arithmetic and copies ran while one was open for 32% -> 22% of each run, Pallas kernels for 0% -> 0%
where the time goes in v1:
time: 1230 us; the launch traced here: 1220 us
  waiting for transfers between devices  553 us (45%)
  local copies, waits for them, and re-layouts  277 us (23%)
  matrix products  208 us (17%)
  other arithmetic  95.4 us (8%)
  blocking collectives  46.7 us (4%)
  starting transfers between devices  21.5 us (2%)
  between operations  16.8 us (1%)
    psum x1, waiting for transfers between devices, per_device(): lax.psum((norm_gain_grad, norm_bias_grad, query_weight_grad, query_bias_g...  402 us
    psum x1, waiting for transfers between devices, per_device(): lax.psum(lax.psum((norm_gain_grad, norm_bias_grad, query_weight_grad, que...  144 us
    dot_general x42, matrix products, contract(): return jnp.einsum(formula, left_side, right_side, precision=highest)  121 us
    dot_general x18, matrix products, matmul(): return jnp.dot(left_side, right_side, precision=highest)  87.1 us
    reshape x12, local copies, waits for them, and re-layouts, per_device(): jnp.repeat(part_num.reshape(groups, span_tokens // stride, heads, head_si...  36.1 us
    psum x1, blocking collectives, per_device(): lax.psum((norm_gain_grad, norm_bias_grad, query_weight_grad, query_bias_g...  34.6 us
    transpose x22, local copies, waits for them, and re-layouts, contract(): return jnp.einsum(formula, left_side, right_side, precision=highest)  27 us
    unnamed x356, local copies, waits for them, and re-layouts  26.9 us
  transfers between devices with their start and end apart: 12, of which 4 were waited for; matrix products, arithmetic and copies ran while one was open for 22% of the time, Pallas kernels for 0%

profile of v1, /device:TPU:0, one launch (start us, length us, event | category | flops | bytes accessed | tf_op | source)
XLA Modules:
  0.0 1218.3 jit_solution(4954011379407517146)
XLA Ops:
  22.9 5.1 reduce_sum.457
  56.2 4.1 fusion.33
  98.7 4.3 fusion.162
  152.0 5.6 reshape.1074
  157.6 15.4 %fusion.161 = (f32[2,16,8,16]{3,2,1,0:T(8,128)S(1)}, f32[2,16,8,16,48]{4,3,2,1,0:T(8,128)}) fusion(f32[16,48]{1,0:T(8,128)S(1)} %and_convert_fusion, f32[2,16,48,8,64]{4,3,2,1,0:T(8,128)} %reshape.1074, f32[2,16,16,8,64]{4,3,2,1,0:T(8,128)} %reshape_reshape.24), kind=kOutput, calls=%fused_computation.291 | convolution fusion | flops 151384064 | bytes 5000192 | tf_op jit(solution)/shard_map/gbqhe,gbkhe->gbhqk/dot_general | solution.py:35
  181.2 4.5 collective-permute-start.3
  185.7 5.6 reshape.1073
  191.3 9.1 fusion.23
  242.8 4.2 add_divide_fusion
  249.6 6.9 fusion.65
  256.6 9.1 fusion.164
  265.7 8.8 fusion.64
  274.5 7.7 multiply_reduce_fusion
  301.8 4.3 multiply_reduce_fusion.3
  308.9 12.6 %convolution_bitcast_fusion = f32[2,16,48,8,64]{4,2,3,1,0:T(8,128)S(1)} fusion(f32[2,16,8,16,48]{4,3,2,1,0:T(8,128)} %get-tuple-element.137, f32[2,16,16,8,64]{4,3,2,1,0:T(8,128)} %reshape.1145, f32[2,16,16,8]{2,3,1,0:T(8,128)S(1)} %get-tuple-element.84), kind=kOutput, calls=%fused_computation.17 | convolution fusion | flops 151257088 | bytes 4997120 | tf_op jit(solution)/shard_map/gbhqk,gbqhe->gbkhe/dot_general | solution.py:35
  321.5 5.2 copy.830
  326.7 6.2 reshape.1182
  332.9 14.5 %add_multiply_fusion.2 = f32[2,16,8,16,48]{4,3,2,1,0:T(8,128)S(1)} fusion(f32[2,16,8,16,48]{4,3,2,1,0:T(8,128)} %get-tuple-element.137, f32[2,16,48,8,64]{4,3,2,1,0:T(8,128)} %reshape.1073, f32[2,16,8,16]{3,2,1,0:T(8,128)} %get-tuple-element.83, f32[2,16,16,8,64]{4,3,2,1,0:T(8,128)} %reshape.1145, f32[2,16,16,8]{2,3,1,0:T(8,128)S(1)} %get-tuple-element.84), kind=kOutput, calls=%fused_computation.25 | convolution fusion | flops 151650304 | bytes 5799936 | tf_op jit(solution)/shard_map/gbqhe,gbkhe->gbhqk/dot_general | solution.py:35
  348.8 10.1 convolution_bitcast_fusion.1
  359.0 5.5 copy.829
  364.5 6.3 reshape.1181
  406.3 4.0 fusion.30
  444.1 10.5 fusion.28
  493.4 7.4 fusion.142
  509.8 4.0 fusion.166
  560.5 3.7 mul.399
  572.6 402.1 %all-reduce.10.cloned.1.call-done = (f32[512,512]{1,0:T(8,128)}, f32[512,512]{1,0:T(8,128)}, f32[512,512]{1,0:T(8,128)}, f32[512,512]{1,0:T(8,128)}, f32[512,2048]{1,0:T(8,128)}, /*index=5*/f32[2048,512]{1,0:T(8,128)}) async-done(((f32[512,512]{1,0:T(8,128)}, f32[512,512]{1,0:T(8,128)}, f32[512,512]{1,0:T(8,128)}, f32[512,512]{1,0:T(8,128)}, f32[512,2048]{1,0:T(8,128)}, /*index=5*/f32[2048,512]{1,0:T(8,128)}), ...) | async-done | bytes 12582928 | tf_op jit(solution)/shard_map/psum | solution.py:337
  978.0 3.8 copy.806
  988.8 10.9 fusion.35
  1006.3 34.6 %all-reduce.3 = (f32[512]{0:T(512)S(1)}, f32[512]{0:T(512)S(1)}, f32[512]{0:T(512)S(1)}, f32[512]{0:T(512)S(1)}, f32[512]{0:T(512)S(1)}, /*index=5*/f32[512]{0:T...) all-reduce(f32[512]{0:T(512)S(1)} %get-tuple-element.43, ...), channel_id=1, replica_groups=mesh['batch'=4,'seq'=8] {'seq'}, use_global_device_ids=true, to_apply=%region_41.42 | all-reduce | flops 6144 | bytes 49152 | tf_op jit(solution)/shard_map/psum | solution.py:337
  1040.9 12.1 all-reduce.5
  1055.6 144.4 %all-reduce.12.cloned.1.call-done = (f32[512,512]{1,0:T(8,128)}, f32[512,512]{1,0:T(8,128)}, f32[512,512]{1,0:T(8,128)}, f32[512,512]{1,0:T(8,128)}, f32[512,2048]{1,0:T(8,128)}, /*index=5*/f32[2048,512]{1,0:T(8,128)}) async-done(((f32[512,512]{1,0:T(8,128)}, f32[512,512]{1,0:T(8,128)}, f32[512,512]{1,0:T(8,128)}, f32[512,512]{1,0:T(8,128)}, f32[512,2048]{1,0:T(8,128)}, /*index=5*/f32[2048,512]{1,0:T(8,128)}), ...) | async-done | bytes 12582928 | tf_op jit(solution)/shard_map/psum | solution.py:336
  (711 shorter events, 408.8 us)
Async XLA Ops:
  7.2 967.5 %all-reduce.10.cloned.1.call-start = ((), (), s32[]{:S(2)}) async-start(), calls=%async_computation | async-start | bytes 25165824 | tf_op jit(solution)/shard_map/psum | solution.py:337
  10.7 45.5 %copy-start.3 = (f32[512,512]{1,0:T(8,128)}, f32[512,512]{1,0:T(8,128)S(1)}, u32[]{:S(2)}) copy-start(f32[512,512]{1,0:T(8,128)S(1)} %fusion.52) | copy-start | bytes 3145732
  42.1 18.2 %copy-start.59 = (f32[2,32,1024]{2,1,0:T(8,128)}, f32[2,32,1024]{2,1,0:T(8,128)S(1)}, u32[]{:S(2)}) copy-start(f32[2,32,1024]{2,1,0:T(8,128)S(1)} %reduce_sum.463) | copy-start | bytes 786436
  46.6 128.9 %collective-permute-start.2 = (f32[2,16,1024]{2,1,0:T(8,128)}, f32[2,16,1024]{2,1,0:T(8,128)}, u32[]{:S(2)}, u32[]{:S(2)}) collective-permute-start(f32[2,16,1024]{2,1,0:T(8,128)} %broadcast_multiply_fusion.9), channel_id=1, source_target_pairs={{0,1},{1,0},{2,3},{3,2},{4,5},{5,4},{6,7},{7,6},{8,9},{9,8},{10,11... | collective-permute-start | bytes 393224 | tf_op jit(solution)/shard_map/ppermute | solution.py:27
  51.3 93.5 %collective-permute-start = (f32[2,16,1024]{2,1,0:T(8,128)}, f32[2,16,1024]{2,1,0:T(8,128)}, u32[]{:S(2)}, u32[]{:S(2)}) collective-permute-start(f32[2,16,1024]{2,1,0:T(8,128)} %get-tuple-element.108), channel_id=1, source_target_pairs={{0,1},{1,2},{2,3},{3,4},{4,5},{5,6},{6,7},{8,9},{9,10},{10,11},{11... | collective-permute-start | bytes 393224 | tf_op jit(solution)/shard_map/ppermute | solution.py:18
  53.8 90.9 %collective-permute-start.1 = (f32[2,16,1024]{2,1,0:T(8,128)}, f32[2,16,1024]{2,1,0:T(8,128)}, u32[]{:S(2)}, u32[]{:S(2)}) collective-permute-start(f32[2,16,1024]{2,1,0:T(8,128)} %get-tuple-element.109), channel_id=1, source_target_pairs={{1,0},{2,1},{3,2},{4,3},{5,4},{6,5},{7,6},{9,8},{10,9},{11,10},{12... | collective-permute-start | bytes 393224 | tf_op jit(solution)/shard_map/ppermute | solution.py:21
  69.3 29.4 %copy-start.17 = (f32[2,128,8,64]{3,2,1,0:T(8,128)}, f32[2,128,8,64]{3,2,1,0:T(8,128)S(1)}, u32[]{:S(2)}) copy-start(f32[2,128,8,64]{3,2,1,0:T(8,128)S(1)} %broadcast_multiply_fusion.1) | copy-start | bytes 1572868
  84.9 91.6 %copy-start.66 = (f32[2,16,8,64]{3,2,1,0:T(8,128)}, f32[2,16,8,64]{3,2,1,0:T(8,128)S(1)}, u32[]{:S(2)}) copy-start(f32[2,16,8,64]{3,2,1,0:T(8,128)S(1)} %reduce_sum.467) | copy-start | bytes 196612
  176.9 28.7 %copy-start.68 = (f32[2,8,16,16]{2,3,1,0:T(8,128)}, f32[2,8,16,16]{2,3,1,0:T(8,128)S(1)}, u32[]{:S(2)}) copy-start(f32[2,8,16,16]{2,3,1,0:T(8,128)S(1)} %get-tuple-element.131) | copy-start | bytes 49156
  181.2 36.7 %collective-permute-start.3 = (f32[2,16,1024]{2,1,0:T(8,128)S(1)}, f32[2,16,1024]{2,1,0:T(8,128)S(1)}, u32[]{:S(2)}, u32[]{:S(2)}) collective-permute-start(f32[2,16,1024]{2,1,0:T(8,128)S(1)} %broadcast_multiply_fusion.8), channel_id=1, source_target_pairs={{0,2},{1,3},{2,0},{3,1},{4,6},{5,7},{6,4},{7,5},{8,10},{9,11},{10,... | collective-permute-start | bytes 393224 | tf_op jit(solution)/shard_map/ppermute | solution.py:27
  218.4 11.8 copy-start.136
  219.8 11.8 collective-permute-start.4
  232.2 74.7 %copy-start.129 = (f32[2,8,4]{1,2,0:T(4,128)}, f32[2,8,4]{1,2,0:T(4,128)S(1)}, u32[]{:S(2)}) copy-start(f32[2,8,4]{1,2,0:T(4,128)S(1)} %copy.712) | copy-start | bytes 772
  332.9 15.9 %copy-start.10 = (f32[2,16,16,8,64]{4,3,2,1,0:T(8,128)S(1)}, f32[2,16,16,8,64]{4,3,2,1,0:T(8,128)}, u32[]{:S(2)}) copy-start(f32[2,16,16,8,64]{4,3,2,1,0:T(8,128)} %reshape_reshape.24) | copy-start | bytes 3145732
  444.1 14.7 %copy-start.47 = (f32[2,8,16,8,64]{4,2,3,1,0:T(8,128)S(1)}, f32[2,8,16,8,64]{4,2,3,1,0:T(8,128)}, u32[]{:S(2)}) copy-start(f32[2,8,16,8,64]{4,2,3,1,0:T(8,128)} %convolution_bitcast_fusion.4) | copy-start | bytes 1572868
  454.6 78.7 %collective-permute-start.8 = (f32[2,16,1024]{2,1,0:T(8,128)}, f32[2,16,1024]{2,1,0:T(8,128)}, u32[]{:S(2)}, u32[]{:S(2)}) collective-permute-start(f32[2,16,1024]{2,1,0:T(8,128)} %get-tuple-element.101), channel_id=1, source_target_pairs={{0,1},{1,2},{2,3},{3,4},{4,5},{5,6},{6,7},{8,9},{9,10},{10,11},{11... | collective-permute-start | bytes 393224 | tf_op jit(solution)/shard_map/ppermute | solution.py:18
  457.5 82.8 %collective-permute-start.9 = (f32[2,16,1024]{2,1,0:T(8,128)}, f32[2,16,1024]{2,1,0:T(8,128)}, u32[]{:S(2)}, u32[]{:S(2)}) collective-permute-start(f32[2,16,1024]{2,1,0:T(8,128)} %get-tuple-element.100), channel_id=1, source_target_pairs={{1,0},{2,1},{3,2},{4,3},{5,4},{6,5},{7,6},{9,8},{10,9},{11,10},{12... | collective-permute-start | bytes 393224 | tf_op jit(solution)/shard_map/ppermute | solution.py:21
  472.1 14.3 %copy-start.69 = (f32[2,8,16,16]{2,3,1,0:T(8,128)S(1)}, f32[2,8,16,16]{2,3,1,0:T(8,128)}, u32[]{:S(2)}) copy-start(f32[2,8,16,16]{2,3,1,0:T(8,128)} %copy-done.68) | copy-start | bytes 49156
  472.1 14.3 %copy-start.75 = (f32[2,16,8,64]{3,2,1,0:T(8,128)S(1)}, f32[2,16,8,64]{3,2,1,0:T(8,128)}, u32[]{:S(2)}) copy-start(f32[2,16,8,64]{3,2,1,0:T(8,128)} %fusion.140) | copy-start | bytes 196612
  472.2 15.9 %copy-start.79 = (f32[2,16,8,64]{3,2,1,0:T(8,128)S(1)}, f32[2,16,8,64]{3,2,1,0:T(8,128)}, u32[]{:S(2)}) copy-start(f32[2,16,8,64]{3,2,1,0:T(8,128)} %copy-done.78) | copy-start | bytes 196612
  472.9 56.5 %collective-permute-start.5 = (f32[2,16,1024]{2,1,0:T(8,128)}, f32[2,16,1024]{2,1,0:T(8,128)}, u32[]{:S(2)}, u32[]{:S(2)}) collective-permute-start(f32[2,16,1024]{2,1,0:T(8,128)} %maximum_bitcast_fusion), channel_id=1, source_target_pairs={{0,4},{1,5},{2,6},{3,7},{4,0},{5,1},{6,2},{7,3},{8,12},{9,13},{10,... | collective-permute-start | bytes 393224 | tf_op jit(solution)/shard_map/ppermute | solution.py:27
  477.4 11.1 copy-start.46
  514.9 12.4 %copy-start.107 = (f32[2,1,16,8,64]{4,2,3,0,1:T(8,128)S(1)}, f32[2,1,16,8,64]{4,2,3,0,1:T(8,128)}, u32[]{:S(2)}) copy-start(f32[2,1,16,8,64]{4,2,3,0,1:T(8,128)} %convolution_bitcast_fusion.16) | copy-start | bytes 196612
  514.9 14.1 %copy-start.67 = (f32[2,16,8,64]{3,2,1,0:T(8,128)S(1)}, f32[2,16,8,64]{3,2,1,0:T(8,128)}, u32[]{:S(2)}) copy-start(f32[2,16,8,64]{3,2,1,0:T(8,128)} %copy-done.66) | copy-start | bytes 196612
  514.9 14.1 %copy-start.86 = (f32[2,8,16,16]{2,3,1,0:T(8,128)S(1)}, f32[2,8,16,16]{2,3,1,0:T(8,128)}, u32[]{:S(2)}) copy-start(f32[2,8,16,16]{2,3,1,0:T(8,128)} %copy-done.85) | copy-start | bytes 49156
  533.1 5.0 collective-permute-start.6
  540.1 5.0 collective-permute-start.7
  572.6 627.5 %all-reduce.12.cloned.1.call-start = ((), (), s32[]{:S(2)}) async-start(), calls=%async_computation.1 | async-start | bytes 25165824 | tf_op jit(solution)/shard_map/psum | solution.py:336
  1002.9 50.1 %copy-start.2 = (f32[2,256,512]{2,1,0:T(8,128)S(1)}, f32[2,256,512]{2,1,0:T(8,128)}, u32[]{:S(2)}) copy-start(f32[2,256,512]{2,1,0:T(8,128)} %param.21) | copy-start | bytes 3145732
  1002.9 50.1 %copy-start.16 = (f32[512,512]{1,0:T(8,128)S(1)}, f32[512,512]{1,0:T(8,128)}, u32[]{:S(2)}) copy-start(f32[512,512]{1,0:T(8,128)} %copy-done.14) | copy-start | bytes 3145732
  1002.9 50.1 %copy-start.152 = (f32[1,2,2,128]{3,1,2,0:T(2,128)S(1)}, f32[1,2,2,128]{3,1,2,0:T(2,128)}, u32[]{:S(2)}) copy-start(f32[1,2,2,128]{3,1,2,0:T(2,128)} %copy-done.151) | copy-start | bytes 6148
  1002.9 50.1 %copy-start.154 = (f32[1,2,2,128]{3,1,2,0:T(2,128)S(1)}, f32[1,2,2,128]{3,1,2,0:T(2,128)}, u32[]{:S(2)}) copy-start(f32[1,2,2,128]{3,1,2,0:T(2,128)} %copy-done.153) | copy-start | bytes 6148
  (152 other events, 629.7 us)
Sparse Core Ops, SparseCore 0:
  572.7 401.9 all-reduce.9
  978.1 221.8 all-reduce.11
